TPU v7x, 256 devices: a whole 4x4x8 slice. The times are simulated.
256 devices in a mesh: seq: 64 (over z, y, core), head: 4 (over x).
Axes of the slice: x: 4, y: 4, z: 8, core: 2. Of those that a mesh axis runs over, the one named last changes fastest.
Arguments:
- queries: bfloat16 [32, 64, 128], P(None, 'head'), may hold values from -12 to 12
- keys: bfloat16 [32, 8, 8192, 128], P(None, 'head', 'seq'), may hold values from -6 to 6
- values: bfloat16 [32, 8, 8192, 128], P(None, 'head', 'seq'), may hold values from -6 to 6
- codes: int32 [32, 8, 32, 8192], P(None, 'head', None, 'seq'), may hold values from 0 to 255
- centroids: float32 [8, 4, 32, 256], P('head'), may hold values from -6 to 6
- picks: int32 [32, 8, 64], P(None, 'head'), may hold values from 0 to 511, as said below
- block_len: int32 [32, 512], P(None, 'seq'), may hold values from 1 to 16
- out_weight: bfloat16 [8192, 8192], P('head', 'seq'), may hold values from -0.0625 to 0.0625
Outputs:
- estimates: float32 [32, 8, 512], P(None, 'head', 'seq')
- attended: bfloat16 [64, 4, 1024], P('seq', 'head')
- layer_out: bfloat16 [32, 8192], P('head', 'seq')
Inputs may be any that keep to these rules, and one draw needn't show every extreme that they name: Each row picks[b, h, :] holds 64 different block numbers in no particular order; among the 8 blocks j * 8 to (j + 1) * 8 - 1 of any j at most 4 are picked, and in every row some j has exactly 4.
All inputs are finite; a program needn't handle non-finite values.
Results may differ from a plain program's by a relative error of at most 0.0049.
Values may be sent and summed in bfloat16 or wider, within the bound.
A program may use at most 64 MiB of HBM per device.

v0:
```python
import jax
import jax.numpy as jnp
from jax import lax
from jax.sharding import PartitionSpec as P

NEG = -1e30


def slot_matrix(sel_rows, shard, nblk_dev, capacity):
    local = sel_rows - shard * nblk_dev
    inside = (local >= 0) & (local < nblk_dev)
    hits = (local[:, :, None] == lax.iota(jnp.int32, nblk_dev)[None, None, :]) & inside[:, :, None]
    taken = jnp.sum(hits.astype(jnp.int32), axis=1)
    position = jnp.cumsum(taken, axis=1) - 1
    place = (position[:, None, :] == lax.iota(jnp.int32, capacity)[None, :, None]) & (
        taken[:, None, :] > 0
    )
    return place.astype(jnp.bfloat16)


def attend(query, keys_s, values_s, lens_s):
    pairs, rows, width = keys_s.shape
    head_dim = query.shape[-1]
    block = width // head_dim
    key_rows = keys_s.reshape(pairs, rows * block, head_dim)
    value_rows = values_s.reshape(pairs, rows * block, head_dim)
    score = jnp.einsum(
        "pgd,ptd->pgt", query, key_rows, preferred_element_type=jnp.float32
    ) * head_dim ** (-0.5)
    live = (
        lax.iota(jnp.int32, block).astype(jnp.float32)[None, None, :]
        < lens_s.astype(jnp.float32)[:, :, None]
    )
    live = live.reshape(pairs, 1, rows * block)
    top = jnp.max(jnp.where(live, score, NEG), axis=2)
    weight = jnp.where(live, jnp.exp(score - top[:, :, None]), 0.0)
    total = jnp.sum(weight, axis=2)
    acc = jnp.einsum(
        "pgt,ptd->pgd", weight, value_rows.astype(jnp.float32), precision=lax.Precision.HIGHEST
    )
    return (top, total, acc)


def fold_rows(top, total, acc):
    best = jnp.max(top, axis=0)
    scale = jnp.exp(top - best[None])
    return (best, jnp.sum(total * scale, axis=0), jnp.sum(acc * scale[..., None], axis=0))


def shards(queries, keys, values, codes, centroids, picks, block_len, out_weight):
    batch, kv_local, seq_local, head_dim = keys.shape
    group = queries.shape[1] // kv_local
    nblk_dev = block_len.shape[1]
    block = seq_local // nblk_dev
    capacity = nblk_dev // 2
    pairs = batch * kv_local
    sub = centroids.shape[1]
    nsub = centroids.shape[2]
    cent = centroids.shape[3]
    shard = lax.axis_index("seq")
    query_float = queries.astype(jnp.float32).reshape(batch, kv_local, group, nsub, sub)
    table = jnp.einsum(
        "bhgms,hsmc->bhgmc", query_float, centroids, precision=lax.Precision.HIGHEST
    ) * head_dim ** (-0.5)
    table = table.astype(jnp.bfloat16).reshape(pairs, group, nsub * cent)
    lens_pair = jnp.repeat(block_len, kv_local, axis=0)
    step_rows = 4
    steps_count = pairs // step_rows

    def score_group(carry, items):
        tab, code, lens = items
        onehot = (code[:, :, None, :] == lax.iota(jnp.int32, cent)[None, None, :, None]).astype(
            jnp.bfloat16
        )
        onehot = onehot.reshape(step_rows, nsub * cent, seq_local)
        approx = jnp.einsum("pgk,pkt->pgt", tab, onehot, preferred_element_type=jnp.float32)
        approx = approx.reshape(step_rows, group, nblk_dev, block)
        live = (lax.iota(jnp.int32, block)[None, None, :] < lens[:, :, None])[:, None]
        top = jnp.max(jnp.where(live, approx, NEG), axis=(1, 3))
        mass = jnp.sum(jnp.where(live, jnp.exp(approx - top[:, None, :, None]), 0.0), axis=(1, 3))
        return (carry, top + jnp.log(mass))

    grouped = (
        table.reshape(steps_count, step_rows, group, nsub * cent),
        codes.reshape(steps_count, step_rows, nsub, seq_local),
        lens_pair.reshape(steps_count, step_rows, nblk_dev),
    )
    unused, estimated = lax.scan(score_group, 0, grouped)
    estimates = estimated.reshape(batch, kv_local, nblk_dev)
    sel_rows = picks.reshape(pairs, picks.shape[-1])
    place = slot_matrix(sel_rows, shard, nblk_dev, capacity)
    key_blocks = keys.reshape(pairs, nblk_dev, block * head_dim)
    value_blocks = values.reshape(pairs, nblk_dev, block * head_dim)
    lens_float = lens_pair.astype(jnp.float32)
    query_all = queries.reshape(pairs, group, head_dim)
    own_query = lax.dynamic_slice_in_dim(query_all, shard, 1, 0)
    send_keys = jnp.einsum(
        "pcn,pnd->cpd", place, key_blocks, preferred_element_type=jnp.float32
    ).astype(jnp.bfloat16)
    send_values = jnp.einsum(
        "pcn,pnd->cpd", place, value_blocks, preferred_element_type=jnp.float32
    ).astype(jnp.bfloat16)
    send_lens = jnp.einsum("pcn,pn->cp", place.astype(jnp.float32), lens_float).astype(jnp.bfloat16)
    got_keys = lax.all_to_all(send_keys, "seq", split_axis=1, concat_axis=1, tiled=True)
    got_values = lax.all_to_all(send_values, "seq", split_axis=1, concat_axis=1, tiled=True)
    got_lens = lax.all_to_all(send_lens, "seq", split_axis=1, concat_axis=1, tiled=True)
    count = got_keys.shape[0]
    query_rep = jnp.broadcast_to(own_query, (count, group, head_dim))
    pieces = attend(query_rep, got_keys, got_values, got_lens)
    top, total, acc = fold_rows(pieces[0], pieces[1], pieces[2])
    head_out = (acc / total[..., None]).astype(jnp.bfloat16)
    attended = head_out.reshape(1, 1, group * head_dim)
    flat = head_out.reshape(1, group * head_dim)
    weight_parts = out_weight.reshape(kv_local, group * head_dim, out_weight.shape[1])
    piece = lax.all_gather(flat, "seq", axis=0, tiled=True)
    products = jnp.einsum("ik,hkd->ihd", piece, weight_parts, preferred_element_type=jnp.float32)
    parity = lax.iota(jnp.int32, piece.shape[0]) % kv_local
    select = (parity[:, None] == lax.iota(jnp.int32, kv_local)[None, :]).astype(jnp.float32)
    gathered = jnp.sum(products * select[:, :, None], axis=1)
    per_request = jnp.sum(gathered.reshape(batch, kv_local, out_weight.shape[1]), axis=1)
    layer_out = lax.psum_scatter(per_request, "head", scatter_dimension=0, tiled=True).astype(
        jnp.bfloat16
    )
    return (estimates, attended, layer_out)


def solution(mesh):
    placed = (
        P(None, "head", None),
        P(None, "head", "seq", None),
        P(None, "head", "seq", None),
        P(None, "head", None, "seq"),
        P("head", None, None, None),
        P(None, "head", None),
        P(None, "seq"),
        P("head", "seq"),
    )
    return jax.shard_map(
        shards,
        mesh=mesh,
        in_specs=placed,
        out_specs=(P(None, "head", "seq"), P("seq", "head", None), P("head", "seq")),
        check_vma=False,
    )
```

profile of v0, /device:TPU:8, one launch (start us, length us, event | category | flops | bytes accessed | tf_op | source)
XLA Modules:
  0.0 276.4 jit_solution(5679206314056601219)
XLA Ops:
  4.7 12.1 %all-to-all-start = ((bf16[4,64,1]{0,2,1:T(2,128)(2,1)}), bf16[4,64,1]{0,2,1:T(2,128)(2,1)S(1)}, u32[]{:S(2)}, u32[]{:S(2)}) async-start(bf16[4,64,1]{0,2,1:T(2,128)(2,1)} %copy.64), calls=%async_computation | async-start | bytes 65536 | tf_op jit(solution)/shard_map/all_to_all | solution.py:106
  16.9 2.8 %reshape.221 = bf16[64,8,2048]{2,1,0:T(8,128)(2,1)S(1)} reshape(bf16[32,2,128,128]{3,2,1,0:T(8,128)(2,1)} %param.11) | data formatting | bytes 4194304 | tf_op jit(solution)/shard_map/reshape | solution.py:92
  19.7 1.7 fusion.5
  21.4 4.0 %all-to-all-done = bf16[4,64,1]{0,2,1:T(2,128)(2,1)S(1)} async-done(((bf16[4,64,1]{0,2,1:T(2,128)(2,1)}), bf16[4,64,1]{0,2,1:T(2,128)(2,1)S(1)}, u32[]{:S(2)}, u32[]{:S(2)}) %all-to-all-start) | async-done | bytes 544 | tf_op jit(solution)/shard_map/all_to_all | solution.py:106
  25.5 6.6 %all-to-all-start.1 = ((bf16[4,64,2048]{2,0,1:T(4,128)(2,1)}), bf16[4,64,2048]{2,0,1:T(4,128)(2,1)}, u32[]{:S(2)}, u32[]{:S(2)}) async-start(bf16[4,64,2048]{2,0,1:T(4,128)(2,1)} %fusion.5), calls=%async_computation.1 | async-start | bytes 2097152 | tf_op jit(solution)/shard_map/all_to_all | solution.py:104
  32.1 2.8 %reshape.223 = bf16[64,8,2048]{2,1,0:T(8,128)(2,1)S(1)} reshape(bf16[32,2,128,128]{3,2,1,0:T(8,128)(2,1)} %param.12) | data formatting | bytes 4194304 | tf_op jit(solution)/shard_map/reshape | solution.py:93
  36.4 9.1 %fusion.4 = bf16[32,2,8,32,256]{4,0,2,3,1:T(8,128)(2,1)} fusion(bf16[32,2,8,32,4]{0,2,1,4,3:T(8,128)(2,1)S(1)} %bitcast.87, f32[2,4,32,256,1]{3,2,1,0,4:T(8,128)S(1)} %bitcast.90), kind=kOutput, calls=%fused_computation.13 | convolution fusion | flops 209715200 | bytes 8781824 | tf_op jit(solution)/shard_map/bhgms,hsmc->bhgmc/dot_general | solution.py:62
  45.5 11.4 %copy.62 = bf16[32,2,8,32,256]{4,3,2,1,0:T(8,128)(2,1)} copy(bf16[32,2,8,32,256]{4,0,2,3,1:T(8,128)(2,1)} %fusion.4) | data formatting | bytes 16777216 | tf_op jit(solution)/shard_map/convert_element_type | solution.py:65
  56.9 13.5 %reshape_reshape.7 = bf16[16,4,8,8192]{3,2,1,0:T(8,128)(2,1)} reshape(bf16[32,2,8,32,256]{4,3,2,1,0:T(8,128)(2,1)} %copy.62) | data formatting | bytes 16777216 | tf_op jit(solution)/shard_map/reshape;reshape | solution.py:84
  70.4 1.8 fusion.6
  72.1 10.3 %all-to-all-start.2 = ((bf16[4,64,2048]{2,0,1:T(4,128)(2,1)}), bf16[4,64,2048]{2,0,1:T(4,128)(2,1)S(1)}, u32[]{:S(2)}, u32[]{:S(2)}) async-start(bf16[4,64,2048]{2,0,1:T(4,128)(2,1)} %fusion.6), calls=%async_computation.2 | async-start | bytes 2097152 | tf_op jit(solution)/shard_map/all_to_all | solution.py:105
  82.5 120.3 %while.10 = (s32[]{:T(128)}, f32[16,4,8]{2,1,0:T(4,128)S(1)}, s32[16,4,8]{2,1,0:T(4,128)S(1)}, bf16[16,4,8,8192]{3,2,1,0:T(8,128)(2,1)}, s32[16,4,32,128]{3,2,1,0:T(8,128)}, /*index=5*/s32[]{:T(128)}, f32[]{:T(128)}, f32[]{:T(128)}) while((s32[]{:T(128)}, f32[16,4,8]{2,1,0:T(4,128)S(1)}, s32[16,4,8]{2,1,0:T(4,128)S(1)}, ...), condition=%wide.region_5.6_spmd, body=%wide.region_0.5_spmd.sunk | while | flops 71324128 | bytes 9317225 | solution.py:88
  83.6 2.7 bitcast_compare_fusion.2
  86.3 3.1 %select_reduce_fusion.6 = (f32[4,128]{1,0:T(4,128)S(1)}, f32[4,8,128]{2,1,0:T(8,128)S(1)}) fusion(pred[4,128]{1,0:T(4,128)(4,1)S(1)} %broadcast_compare_fusion.4, pred[4,8192,128]{2,1,0:T(32,128)(4,1)S(1)} %bitcast_compare_fusion.2, bf16[16,4,8,8192]{3,2,1,0:T(8,128)(2,1)} %get-tuple-element.121, s32[]{:T(128)} %get-tuple-element.110), kind=kOutput, calls=%fused_computation.7.clone.1 | convolution fusion | flops 67116544 | bytes 4738048 | tf_op jit(solution)/shard_map/while/body/eval_jaxpr/pgk,pkt->pgt/dot_general | solution.py:76
  91.2 2.7 bitcast_compare_fusion.2
  93.8 3.1 %select_reduce_fusion.6 = (f32[4,128]{1,0:T(4,128)S(1)}, f32[4,8,128]{2,1,0:T(8,128)S(1)}) fusion(pred[4,128]{1,0:T(4,128)(4,1)S(1)} %broadcast_compare_fusion.4, pred[4,8192,128]{2,1,0:T(32,128)(4,1)S(1)} %bitcast_compare_fusion.2, bf16[16,4,8,8192]{3,2,1,0:T(8,128)(2,1)} %get-tuple-element.121, s32[]{:T(128)} %get-tuple-element.110), kind=kOutput, calls=%fused_computation.7.clone.1 | convolution fusion | flops 67116544 | bytes 4738048 | tf_op jit(solution)/shard_map/while/body/eval_jaxpr/pgk,pkt->pgt/dot_general | solution.py:76
  98.7 2.7 bitcast_compare_fusion.2
  101.3 3.1 %select_reduce_fusion.6 = (f32[4,128]{1,0:T(4,128)S(1)}, f32[4,8,128]{2,1,0:T(8,128)S(1)}) fusion(pred[4,128]{1,0:T(4,128)(4,1)S(1)} %broadcast_compare_fusion.4, pred[4,8192,128]{2,1,0:T(32,128)(4,1)S(1)} %bitcast_compare_fusion.2, bf16[16,4,8,8192]{3,2,1,0:T(8,128)(2,1)} %get-tuple-element.121, s32[]{:T(128)} %get-tuple-element.110), kind=kOutput, calls=%fused_computation.7.clone.1 | convolution fusion | flops 67116544 | bytes 4738048 | tf_op jit(solution)/shard_map/while/body/eval_jaxpr/pgk,pkt->pgt/dot_general | solution.py:76
  106.2 2.7 bitcast_compare_fusion.2
  108.9 3.1 %select_reduce_fusion.6 = (f32[4,128]{1,0:T(4,128)S(1)}, f32[4,8,128]{2,1,0:T(8,128)S(1)}) fusion(pred[4,128]{1,0:T(4,128)(4,1)S(1)} %broadcast_compare_fusion.4, pred[4,8192,128]{2,1,0:T(32,128)(4,1)S(1)} %bitcast_compare_fusion.2, bf16[16,4,8,8192]{3,2,1,0:T(8,128)(2,1)} %get-tuple-element.121, s32[]{:T(128)} %get-tuple-element.110), kind=kOutput, calls=%fused_computation.7.clone.1 | convolution fusion | flops 67116544 | bytes 4738048 | tf_op jit(solution)/shard_map/while/body/eval_jaxpr/pgk,pkt->pgt/dot_general | solution.py:76
  113.7 2.7 bitcast_compare_fusion.2
  116.4 3.1 %select_reduce_fusion.6 = (f32[4,128]{1,0:T(4,128)S(1)}, f32[4,8,128]{2,1,0:T(8,128)S(1)}) fusion(pred[4,128]{1,0:T(4,128)(4,1)S(1)} %broadcast_compare_fusion.4, pred[4,8192,128]{2,1,0:T(32,128)(4,1)S(1)} %bitcast_compare_fusion.2, bf16[16,4,8,8192]{3,2,1,0:T(8,128)(2,1)} %get-tuple-element.121, s32[]{:T(128)} %get-tuple-element.110), kind=kOutput, calls=%fused_computation.7.clone.1 | convolution fusion | flops 67116544 | bytes 4738048 | tf_op jit(solution)/shard_map/while/body/eval_jaxpr/pgk,pkt->pgt/dot_general | solution.py:76
  121.2 2.7 bitcast_compare_fusion.2
  123.9 3.1 %select_reduce_fusion.6 = (f32[4,128]{1,0:T(4,128)S(1)}, f32[4,8,128]{2,1,0:T(8,128)S(1)}) fusion(pred[4,128]{1,0:T(4,128)(4,1)S(1)} %broadcast_compare_fusion.4, pred[4,8192,128]{2,1,0:T(32,128)(4,1)S(1)} %bitcast_compare_fusion.2, bf16[16,4,8,8192]{3,2,1,0:T(8,128)(2,1)} %get-tuple-element.121, s32[]{:T(128)} %get-tuple-element.110), kind=kOutput, calls=%fused_computation.7.clone.1 | convolution fusion | flops 67116544 | bytes 4738048 | tf_op jit(solution)/shard_map/while/body/eval_jaxpr/pgk,pkt->pgt/dot_general | solution.py:76
  128.7 2.7 bitcast_compare_fusion.2
  131.4 3.1 %select_reduce_fusion.6 = (f32[4,128]{1,0:T(4,128)S(1)}, f32[4,8,128]{2,1,0:T(8,128)S(1)}) fusion(pred[4,128]{1,0:T(4,128)(4,1)S(1)} %broadcast_compare_fusion.4, pred[4,8192,128]{2,1,0:T(32,128)(4,1)S(1)} %bitcast_compare_fusion.2, bf16[16,4,8,8192]{3,2,1,0:T(8,128)(2,1)} %get-tuple-element.121, s32[]{:T(128)} %get-tuple-element.110), kind=kOutput, calls=%fused_computation.7.clone.1 | convolution fusion | flops 67116544 | bytes 4738048 | tf_op jit(solution)/shard_map/while/body/eval_jaxpr/pgk,pkt->pgt/dot_general | solution.py:76
  136.3 2.7 bitcast_compare_fusion.2
  138.9 3.1 %select_reduce_fusion.6 = (f32[4,128]{1,0:T(4,128)S(1)}, f32[4,8,128]{2,1,0:T(8,128)S(1)}) fusion(pred[4,128]{1,0:T(4,128)(4,1)S(1)} %broadcast_compare_fusion.4, pred[4,8192,128]{2,1,0:T(32,128)(4,1)S(1)} %bitcast_compare_fusion.2, bf16[16,4,8,8192]{3,2,1,0:T(8,128)(2,1)} %get-tuple-element.121, s32[]{:T(128)} %get-tuple-element.110), kind=kOutput, calls=%fused_computation.7.clone.1 | convolution fusion | flops 67116544 | bytes 4738048 | tf_op jit(solution)/shard_map/while/body/eval_jaxpr/pgk,pkt->pgt/dot_general | solution.py:76
  143.8 2.7 bitcast_compare_fusion.2
  146.5 3.1 %select_reduce_fusion.6 = (f32[4,128]{1,0:T(4,128)S(1)}, f32[4,8,128]{2,1,0:T(8,128)S(1)}) fusion(pred[4,128]{1,0:T(4,128)(4,1)S(1)} %broadcast_compare_fusion.4, pred[4,8192,128]{2,1,0:T(32,128)(4,1)S(1)} %bitcast_compare_fusion.2, bf16[16,4,8,8192]{3,2,1,0:T(8,128)(2,1)} %get-tuple-element.121, s32[]{:T(128)} %get-tuple-element.110), kind=kOutput, calls=%fused_computation.7.clone.1 | convolution fusion | flops 67116544 | bytes 4738048 | tf_op jit(solution)/shard_map/while/body/eval_jaxpr/pgk,pkt->pgt/dot_general | solution.py:76
  151.3 2.7 bitcast_compare_fusion.2
  154.0 3.1 %select_reduce_fusion.6 = (f32[4,128]{1,0:T(4,128)S(1)}, f32[4,8,128]{2,1,0:T(8,128)S(1)}) fusion(pred[4,128]{1,0:T(4,128)(4,1)S(1)} %broadcast_compare_fusion.4, pred[4,8192,128]{2,1,0:T(32,128)(4,1)S(1)} %bitcast_compare_fusion.2, bf16[16,4,8,8192]{3,2,1,0:T(8,128)(2,1)} %get-tuple-element.121, s32[]{:T(128)} %get-tuple-element.110), kind=kOutput, calls=%fused_computation.7.clone.1 | convolution fusion | flops 67116544 | bytes 4738048 | tf_op jit(solution)/shard_map/while/body/eval_jaxpr/pgk,pkt->pgt/dot_general | solution.py:76
  158.8 2.7 bitcast_compare_fusion.2
  161.5 3.1 %select_reduce_fusion.6 = (f32[4,128]{1,0:T(4,128)S(1)}, f32[4,8,128]{2,1,0:T(8,128)S(1)}) fusion(pred[4,128]{1,0:T(4,128)(4,1)S(1)} %broadcast_compare_fusion.4, pred[4,8192,128]{2,1,0:T(32,128)(4,1)S(1)} %bitcast_compare_fusion.2, bf16[16,4,8,8192]{3,2,1,0:T(8,128)(2,1)} %get-tuple-element.121, s32[]{:T(128)} %get-tuple-element.110), kind=kOutput, calls=%fused_computation.7.clone.1 | convolution fusion | flops 67116544 | bytes 4738048 | tf_op jit(solution)/shard_map/while/body/eval_jaxpr/pgk,pkt->pgt/dot_general | solution.py:76
  166.3 2.7 bitcast_compare_fusion.2
  169.0 3.1 %select_reduce_fusion.6 = (f32[4,128]{1,0:T(4,128)S(1)}, f32[4,8,128]{2,1,0:T(8,128)S(1)}) fusion(pred[4,128]{1,0:T(4,128)(4,1)S(1)} %broadcast_compare_fusion.4, pred[4,8192,128]{2,1,0:T(32,128)(4,1)S(1)} %bitcast_compare_fusion.2, bf16[16,4,8,8192]{3,2,1,0:T(8,128)(2,1)} %get-tuple-element.121, s32[]{:T(128)} %get-tuple-element.110), kind=kOutput, calls=%fused_computation.7.clone.1 | convolution fusion | flops 67116544 | bytes 4738048 | tf_op jit(solution)/shard_map/while/body/eval_jaxpr/pgk,pkt->pgt/dot_general | solution.py:76
  173.9 2.7 bitcast_compare_fusion.2
  176.5 3.1 %select_reduce_fusion.6 = (f32[4,128]{1,0:T(4,128)S(1)}, f32[4,8,128]{2,1,0:T(8,128)S(1)}) fusion(pred[4,128]{1,0:T(4,128)(4,1)S(1)} %broadcast_compare_fusion.4, pred[4,8192,128]{2,1,0:T(32,128)(4,1)S(1)} %bitcast_compare_fusion.2, bf16[16,4,8,8192]{3,2,1,0:T(8,128)(2,1)} %get-tuple-element.121, s32[]{:T(128)} %get-tuple-element.110), kind=kOutput, calls=%fused_computation.7.clone.1 | convolution fusion | flops 67116544 | bytes 4738048 | tf_op jit(solution)/shard_map/while/body/eval_jaxpr/pgk,pkt->pgt/dot_general | solution.py:76
  181.4 2.7 bitcast_compare_fusion.2
  184.0 3.1 %select_reduce_fusion.6 = (f32[4,128]{1,0:T(4,128)S(1)}, f32[4,8,128]{2,1,0:T(8,128)S(1)}) fusion(pred[4,128]{1,0:T(4,128)(4,1)S(1)} %broadcast_compare_fusion.4, pred[4,8192,128]{2,1,0:T(32,128)(4,1)S(1)} %bitcast_compare_fusion.2, bf16[16,4,8,8192]{3,2,1,0:T(8,128)(2,1)} %get-tuple-element.121, s32[]{:T(128)} %get-tuple-element.110), kind=kOutput, calls=%fused_computation.7.clone.1 | convolution fusion | flops 67116544 | bytes 4738048 | tf_op jit(solution)/shard_map/while/body/eval_jaxpr/pgk,pkt->pgt/dot_general | solution.py:76
  188.9 2.7 bitcast_compare_fusion.2
  191.6 3.1 %select_reduce_fusion.6 = (f32[4,128]{1,0:T(4,128)S(1)}, f32[4,8,128]{2,1,0:T(8,128)S(1)}) fusion(pred[4,128]{1,0:T(4,128)(4,1)S(1)} %broadcast_compare_fusion.4, pred[4,8192,128]{2,1,0:T(32,128)(4,1)S(1)} %bitcast_compare_fusion.2, bf16[16,4,8,8192]{3,2,1,0:T(8,128)(2,1)} %get-tuple-element.121, s32[]{:T(128)} %get-tuple-element.110), kind=kOutput, calls=%fused_computation.7.clone.1 | convolution fusion | flops 67116544 | bytes 4738048 | tf_op jit(solution)/shard_map/while/body/eval_jaxpr/pgk,pkt->pgt/dot_general | solution.py:76
  196.4 2.7 bitcast_compare_fusion.2
  199.1 3.1 %select_reduce_fusion.6 = (f32[4,128]{1,0:T(4,128)S(1)}, f32[4,8,128]{2,1,0:T(8,128)S(1)}) fusion(pred[4,128]{1,0:T(4,128)(4,1)S(1)} %broadcast_compare_fusion.4, pred[4,8192,128]{2,1,0:T(32,128)(4,1)S(1)} %bitcast_compare_fusion.2, bf16[16,4,8,8192]{3,2,1,0:T(8,128)(2,1)} %get-tuple-element.121, s32[]{:T(128)} %get-tuple-element.110), kind=kOutput, calls=%fused_computation.7.clone.1 | convolution fusion | flops 67116544 | bytes 4738048 | tf_op jit(solution)/shard_map/while/body/eval_jaxpr/pgk,pkt->pgt/dot_general | solution.py:76
  205.8 2.8 %copy.66 = bf16[4,64,2048]{2,1,0:T(8,128)(2,1)} copy(bf16[4,64,2048]{2,0,1:T(4,128)(2,1)} %all-to-all-done.1) | data formatting | bytes 2097152 | tf_op jit(solution)/shard_map/all_to_all | solution.py:104
  210.2 1.6 copy.67
  214.7 43.9 %all-gather = bf16[64,1,1024]{2,1,0:T(2,128)(2,1)S(1)} all-gather(bf16[1,1,1024]{2,1,0:T(2,128)(2,1)S(1)} %convert_element_type.94), channel_id=1, replica_groups=mesh['seq'=64,'head'=4] {'seq'}, dimensions={0}, use_global_device_ids=true | all-gather | bytes 133120 | tf_op jit(solution)/shard_map/all_gather | solution.py:115
  258.9 16.9 %all-reduce = bf16[32,128]{1,0:T(8,128)(2,1)S(1)} all-reduce(f32[32,128]{1,0:T(8,128)S(1)} %reduce_sum.75), channel_id=2, replica_groups=mesh['seq'=64,'head'=4] {'head'}, use_global_device_ids=true, to_apply=%region_15.16.clone | all-reduce | flops 4096 | bytes 24576
  (326 shorter events, 40.0 us)
Async XLA Ops:
  0.6 258.0 %copy-start = (bf16[2048,128]{1,0:T(8,128)(2,1)S(1)}, bf16[2048,128]{1,0:T(8,128)(2,1)}, u32[]{:S(2)}) copy-start(bf16[2048,128]{1,0:T(8,128)(2,1)} %param.17) | copy-start | bytes 1572868
  4.7 20.7 %all-to-all-start = ((bf16[4,64,1]{0,2,1:T(2,128)(2,1)}), bf16[4,64,1]{0,2,1:T(2,128)(2,1)S(1)}, u32[]{:S(2)}, u32[]{:S(2)}) async-start(bf16[4,64,1]{0,2,1:T(2,128)(2,1)} %copy.64), calls=%async_computation | async-start | bytes 65536 | tf_op jit(solution)/shard_map/all_to_all | solution.py:106
  16.8 15.2 %copy-start.3 = (s32[32,8]{0,1:T(8,128)S(1)}, s32[32,8]{0,1:T(8,128)}, u32[]{:S(2)}) copy-start(s32[32,8]{0,1:T(8,128)} %param.16) | copy-start | bytes 3076
  21.4 15.0 %copy-start.1 = (f32[2,4,32,256]{3,2,1,0:T(8,128)S(1)}, f32[2,4,32,256]{3,2,1,0:T(8,128)}, u32[]{:S(2)}) copy-start(f32[2,4,32,256]{3,2,1,0:T(8,128)} %param.14) | copy-start | bytes 786436
  25.5 46.7 %all-to-all-start.1 = ((bf16[4,64,2048]{2,0,1:T(4,128)(2,1)}), bf16[4,64,2048]{2,0,1:T(4,128)(2,1)}, u32[]{:S(2)}, u32[]{:S(2)}) async-start(bf16[4,64,2048]{2,0,1:T(4,128)(2,1)} %fusion.5), calls=%async_computation.1 | async-start | bytes 2097152 | tf_op jit(solution)/shard_map/all_to_all | solution.py:104
  72.1 138.0 %all-to-all-start.2 = ((bf16[4,64,2048]{2,0,1:T(4,128)(2,1)}), bf16[4,64,2048]{2,0,1:T(4,128)(2,1)S(1)}, u32[]{:S(2)}, u32[]{:S(2)}) async-start(bf16[4,64,2048]{2,0,1:T(4,128)(2,1)} %fusion.6), calls=%async_computation.2 | async-start | bytes 2097152 | tf_op jit(solution)/shard_map/all_to_all | solution.py:105
  82.5 121.1 %copy-start.4 = (u32[256]{0:T(256)S(1)}, u32[256]{0:T(256)}, u32[]{:S(2)}) copy-start(u32[256]{0:T(256)} %constant.73) | copy-start | bytes 3076
  214.7 61.7 %copy-start.2 = (bf16[1,1,1024]{2,1,0:T(2,128)(2,1)}, bf16[1,1,1024]{2,1,0:T(2,128)(2,1)S(1)}, u32[]{:S(2)}) copy-start(bf16[1,1,1024]{2,1,0:T(2,128)(2,1)S(1)} %convert_element_type.94) | copy-start | bytes 6148
where the time goes:
time: 279 us; the launch traced here: 276 us
  local copies, waits for them, and re-layouts  66.1 us (24%)
  matrix products  64.2 us (23%)
  blocking collectives  60.9 us (22%)
  other arithmetic  49.9 us (18%)
  starting transfers between devices  29 us (10%)
  waiting for transfers between devices  4.04 us (1%)
    dot_general x16, matrix products, score_group(): jnp.einsum('pgk,pkt->pgt', tab, onehot, preferred_element_type=jnp.float32)  50.1 us
    all_gather x1, blocking collectives, shards(): piece = lax.all_gather(flat, 'seq', axis=0, tiled=True)  43.9 us
    eq x16, other arithmetic, score_group(): code[:, :, None, :] == lax.iota(jnp.int32, cent)[None, None, :, None]  42.6 us
    unnamed x1, blocking collectives  16.9 us
    eq x16, local copies, waits for them, and re-layouts, score_group(): code[:, :, None, :] == lax.iota(jnp.int32, cent)[None, None, :, None]  13.6 us
    another operation x1, local copies, waits for them, and re-layouts, shards(): table.reshape(steps_count, step_rows, group, nsub * cent)  13.5 us
    all_to_all x1, starting transfers between devices, shards(): lax.all_to_all(send_lens, 'seq', split_axis=1, concat_axis=1, tiled=True)  12.1 us
    convert_element_type x1, local copies, waits for them, and re-layouts, shards(): table = table.astype(jnp.bfloat16).reshape(pairs, group, nsub * cent)  11.4 us
  transfers between devices with their start and end apart: 3, of which 1 were waited for; matrix products, arithmetic and copies ran while one was open for 62% of the time, Pallas kernels for 0%

commit v1 on v0

--- a/solution.py
+++ b/solution.py
@@ -112,7 +112,8 @@
     attended = head_out.reshape(1, 1, group * head_dim)
     flat = head_out.reshape(1, group * head_dim)
     weight_parts = out_weight.reshape(kv_local, group * head_dim, out_weight.shape[1])
-    piece = lax.all_gather(flat, "seq", axis=0, tiled=True)
+    stack = jnp.stack([flat] * lax.axis_size("seq"))
+    piece = jnp.concatenate(lax.all_to_all(stack, "seq", 0, 0), axis=0)
     products = jnp.einsum("ik,hkd->ihd", piece, weight_parts, preferred_element_type=jnp.float32)
     parity = lax.iota(jnp.int32, piece.shape[0]) % kv_local
     select = (parity[:, None] == lax.iota(jnp.int32, kv_local)[None, :]).astype(jnp.float32)

time: 279 us -> 256 us (0.918)
  blocking collectives: 60.9 us -> 16.9 us
  starting transfers between devices: 29 us -> 39.3 us
  waiting for transfers between devices: 4.04 us -> 11.4 us
    all_gather x1 -> x0, blocking collectives: 43.9 us -> none  [shards(): piece = lax.all_gather(flat, 'seq', axis=0, tiled=True)]
    all_to_all x0 -> x1, starting transfers between devices: none -> 10.3 us  [shards(): piece = jnp.concatenate(lax.all_to_all(stack, 'seq', 0, 0), axis=0)]
    all_to_all x0 -> x1, waiting for transfers between devices: none -> 7.31 us  [shards(): piece = jnp.concatenate(lax.all_to_all(stack, 'seq', 0, 0), axis=0)]
  transfers between devices with their start and end apart: 3 -> 4, of which waited for: 1 -> 2; matrix products, arithmetic and copies ran while one was open for 62% -> 68% of each run, Pallas kernels for 0% -> 0%
where the time goes in v1:
time: 256 us; the launch traced here: 254 us
  local copies, waits for them, and re-layouts  68.2 us (27%)
  matrix products  64.2 us (25%)
  other arithmetic  51.4 us (20%)
  starting transfers between devices  39.3 us (15%)
  blocking collectives  16.9 us (7%)
  waiting for transfers between devices  11.4 us (4%)
    dot_general x16, matrix products, score_group(): jnp.einsum('pgk,pkt->pgt', tab, onehot, preferred_element_type=jnp.float32)  50.1 us
    eq x16, other arithmetic, score_group(): code[:, :, None, :] == lax.iota(jnp.int32, cent)[None, None, :, None]  42.6 us
    unnamed x1, blocking collectives  16.9 us
    eq x16, local copies, waits for them, and re-layouts, score_group(): code[:, :, None, :] == lax.iota(jnp.int32, cent)[None, None, :, None]  13.6 us
    another operation x1, local copies, waits for them, and re-layouts, shards(): table.reshape(steps_count, step_rows, group, nsub * cent)  13.5 us
    all_to_all x1, starting transfers between devices, shards(): lax.all_to_all(send_lens, 'seq', split_axis=1, concat_axis=1, tiled=True)  12.1 us
    convert_element_type x1, local copies, waits for them, and re-layouts, shards(): table = table.astype(jnp.bfloat16).reshape(pairs, group, nsub * cent)  11.4 us
    all_to_all x1, starting transfers between devices, shards(): lax.all_to_all(send_values, 'seq', split_axis=1, concat_axis=1, tiled=True)  10.3 us
  transfers between devices with their start and end apart: 4, of which 2 were waited for; matrix products, arithmetic and copies ran while one was open for 68% of the time, Pallas kernels for 0%

profile of v1, /device:TPU:8, one launch (start us, length us, event | category | flops | bytes accessed | tf_op | source)
XLA Modules:
  0.0 253.6 jit_solution(2183667334936739245)
XLA Ops:
  4.7 12.1 %all-to-all-start = ((bf16[4,64,1]{0,2,1:T(2,128)(2,1)}), bf16[4,64,1]{0,2,1:T(2,128)(2,1)S(1)}, u32[]{:S(2)}, u32[]{:S(2)}) async-start(bf16[4,64,1]{0,2,1:T(2,128)(2,1)} %copy.62), calls=%async_computation | async-start | bytes 65536 | tf_op jit(solution)/shard_map/all_to_all | solution.py:106
  16.9 2.8 %reshape.214 = bf16[64,8,2048]{2,1,0:T(8,128)(2,1)S(1)} reshape(bf16[32,2,128,128]{3,2,1,0:T(8,128)(2,1)} %param.11) | data formatting | bytes 4194304 | tf_op jit(solution)/shard_map/reshape | solution.py:92
  19.7 1.7 fusion.5
  21.4 4.0 %all-to-all-done = bf16[4,64,1]{0,2,1:T(2,128)(2,1)S(1)} async-done(((bf16[4,64,1]{0,2,1:T(2,128)(2,1)}), bf16[4,64,1]{0,2,1:T(2,128)(2,1)S(1)}, u32[]{:S(2)}, u32[]{:S(2)}) %all-to-all-start) | async-done | bytes 544 | tf_op jit(solution)/shard_map/all_to_all | solution.py:106
  25.5 6.6 %all-to-all-start.1 = ((bf16[4,64,2048]{2,0,1:T(4,128)(2,1)}), bf16[4,64,2048]{2,0,1:T(4,128)(2,1)}, u32[]{:S(2)}, u32[]{:S(2)}) async-start(bf16[4,64,2048]{2,0,1:T(4,128)(2,1)} %fusion.5), calls=%async_computation.1 | async-start | bytes 2097152 | tf_op jit(solution)/shard_map/all_to_all | solution.py:104
  32.1 2.8 %reshape.216 = bf16[64,8,2048]{2,1,0:T(8,128)(2,1)S(1)} reshape(bf16[32,2,128,128]{3,2,1,0:T(8,128)(2,1)} %param.12) | data formatting | bytes 4194304 | tf_op jit(solution)/shard_map/reshape | solution.py:93
  36.4 9.1 %fusion.4 = bf16[32,2,8,32,256]{4,0,2,3,1:T(8,128)(2,1)} fusion(bf16[32,2,8,32,4]{0,2,1,4,3:T(8,128)(2,1)S(1)} %bitcast.89, f32[2,4,32,256,1]{3,2,1,0,4:T(8,128)S(1)} %bitcast.92), kind=kOutput, calls=%fused_computation.13 | convolution fusion | flops 209715200 | bytes 8781824 | tf_op jit(solution)/shard_map/bhgms,hsmc->bhgmc/dot_general | solution.py:62
  45.5 11.4 %copy.60 = bf16[32,2,8,32,256]{4,3,2,1,0:T(8,128)(2,1)} copy(bf16[32,2,8,32,256]{4,0,2,3,1:T(8,128)(2,1)} %fusion.4) | data formatting | bytes 16777216 | tf_op jit(solution)/shard_map/convert_element_type | solution.py:65
  56.9 13.5 %reshape_reshape.7 = bf16[16,4,8,8192]{3,2,1,0:T(8,128)(2,1)} reshape(bf16[32,2,8,32,256]{4,3,2,1,0:T(8,128)(2,1)} %copy.60) | data formatting | bytes 16777216 | tf_op jit(solution)/shard_map/reshape;reshape | solution.py:84
  70.4 1.8 fusion.6
  72.1 10.3 %all-to-all-start.2 = ((bf16[4,64,2048]{2,0,1:T(4,128)(2,1)}), bf16[4,64,2048]{2,0,1:T(4,128)(2,1)S(1)}, u32[]{:S(2)}, u32[]{:S(2)}) async-start(bf16[4,64,2048]{2,0,1:T(4,128)(2,1)} %fusion.6), calls=%async_computation.2 | async-start | bytes 2097152 | tf_op jit(solution)/shard_map/all_to_all | solution.py:105
  82.5 120.3 %while.10 = (s32[]{:T(128)}, f32[16,4,8]{2,1,0:T(4,128)S(1)}, s32[16,4,8]{2,1,0:T(4,128)S(1)}, bf16[16,4,8,8192]{3,2,1,0:T(8,128)(2,1)}, s32[16,4,32,128]{3,2,1,0:T(8,128)}, /*index=5*/s32[]{:T(128)}, f32[]{:T(128)}, f32[]{:T(128)}) while((s32[]{:T(128)}, f32[16,4,8]{2,1,0:T(4,128)S(1)}, s32[16,4,8]{2,1,0:T(4,128)S(1)}, ...), condition=%wide.region_5.6_spmd, body=%wide.region_0.5_spmd.sunk | while | flops 71324128 | bytes 9317225 | solution.py:88
  83.6 2.7 %bitcast_compare_fusion.2 = pred[4,8192,128]{2,1,0:T(32,128)(4,1)S(1)} fusion(s32[8192]{0:T(1024)S(1)} %bitcast.88, s32[4,32,128]{2,1,0:T(8,128)S(1)} %dynamic-slice_bitcast_fusion.6), kind=kLoop, calls=%fused_computation.clone.1 | loop fusion | flops 4194304 | bytes 4292608 | tf_op jit(solution)/shard_map/while/body/eval_jaxpr/eq | solution.py:72
  86.3 3.1 %select_reduce_fusion.6 = (f32[4,128]{1,0:T(4,128)S(1)}, f32[4,8,128]{2,1,0:T(8,128)S(1)}) fusion(pred[4,128]{1,0:T(4,128)(4,1)S(1)} %broadcast_compare_fusion.4, pred[4,8192,128]{2,1,0:T(32,128)(4,1)S(1)} %bitcast_compare_fusion.2, bf16[16,4,8,8192]{3,2,1,0:T(8,128)(2,1)} %get-tuple-element.118, s32[]{:T(128)} %get-tuple-element.107), kind=kOutput, calls=%fused_computation.7.clone.1 | convolution fusion | flops 67116544 | bytes 4738048 | tf_op jit(solution)/shard_map/while/body/eval_jaxpr/pgk,pkt->pgt/dot_general | solution.py:76
  91.1 2.7 %bitcast_compare_fusion.2 = pred[4,8192,128]{2,1,0:T(32,128)(4,1)S(1)} fusion(s32[8192]{0:T(1024)S(1)} %bitcast.88, s32[4,32,128]{2,1,0:T(8,128)S(1)} %dynamic-slice_bitcast_fusion.6), kind=kLoop, calls=%fused_computation.clone.1 | loop fusion | flops 4194304 | bytes 4292608 | tf_op jit(solution)/shard_map/while/body/eval_jaxpr/eq | solution.py:72
  93.8 3.1 %select_reduce_fusion.6 = (f32[4,128]{1,0:T(4,128)S(1)}, f32[4,8,128]{2,1,0:T(8,128)S(1)}) fusion(pred[4,128]{1,0:T(4,128)(4,1)S(1)} %broadcast_compare_fusion.4, pred[4,8192,128]{2,1,0:T(32,128)(4,1)S(1)} %bitcast_compare_fusion.2, bf16[16,4,8,8192]{3,2,1,0:T(8,128)(2,1)} %get-tuple-element.118, s32[]{:T(128)} %get-tuple-element.107), kind=kOutput, calls=%fused_computation.7.clone.1 | convolution fusion | flops 67116544 | bytes 4738048 | tf_op jit(solution)/shard_map/while/body/eval_jaxpr/pgk,pkt->pgt/dot_general | solution.py:76
  98.7 2.7 %bitcast_compare_fusion.2 = pred[4,8192,128]{2,1,0:T(32,128)(4,1)S(1)} fusion(s32[8192]{0:T(1024)S(1)} %bitcast.88, s32[4,32,128]{2,1,0:T(8,128)S(1)} %dynamic-slice_bitcast_fusion.6), kind=kLoop, calls=%fused_computation.clone.1 | loop fusion | flops 4194304 | bytes 4292608 | tf_op jit(solution)/shard_map/while/body/eval_jaxpr/eq | solution.py:72
  101.3 3.1 %select_reduce_fusion.6 = (f32[4,128]{1,0:T(4,128)S(1)}, f32[4,8,128]{2,1,0:T(8,128)S(1)}) fusion(pred[4,128]{1,0:T(4,128)(4,1)S(1)} %broadcast_compare_fusion.4, pred[4,8192,128]{2,1,0:T(32,128)(4,1)S(1)} %bitcast_compare_fusion.2, bf16[16,4,8,8192]{3,2,1,0:T(8,128)(2,1)} %get-tuple-element.118, s32[]{:T(128)} %get-tuple-element.107), kind=kOutput, calls=%fused_computation.7.clone.1 | convolution fusion | flops 67116544 | bytes 4738048 | tf_op jit(solution)/shard_map/while/body/eval_jaxpr/pgk,pkt->pgt/dot_general | solution.py:76
  106.2 2.7 %bitcast_compare_fusion.2 = pred[4,8192,128]{2,1,0:T(32,128)(4,1)S(1)} fusion(s32[8192]{0:T(1024)S(1)} %bitcast.88, s32[4,32,128]{2,1,0:T(8,128)S(1)} %dynamic-slice_bitcast_fusion.6), kind=kLoop, calls=%fused_computation.clone.1 | loop fusion | flops 4194304 | bytes 4292608 | tf_op jit(solution)/shard_map/while/body/eval_jaxpr/eq | solution.py:72
  108.9 3.1 %select_reduce_fusion.6 = (f32[4,128]{1,0:T(4,128)S(1)}, f32[4,8,128]{2,1,0:T(8,128)S(1)}) fusion(pred[4,128]{1,0:T(4,128)(4,1)S(1)} %broadcast_compare_fusion.4, pred[4,8192,128]{2,1,0:T(32,128)(4,1)S(1)} %bitcast_compare_fusion.2, bf16[16,4,8,8192]{3,2,1,0:T(8,128)(2,1)} %get-tuple-element.118, s32[]{:T(128)} %get-tuple-element.107), kind=kOutput, calls=%fused_computation.7.clone.1 | convolution fusion | flops 67116544 | bytes 4738048 | tf_op jit(solution)/shard_map/while/body/eval_jaxpr/pgk,pkt->pgt/dot_general | solution.py:76
  113.7 2.7 %bitcast_compare_fusion.2 = pred[4,8192,128]{2,1,0:T(32,128)(4,1)S(1)} fusion(s32[8192]{0:T(1024)S(1)} %bitcast.88, s32[4,32,128]{2,1,0:T(8,128)S(1)} %dynamic-slice_bitcast_fusion.6), kind=kLoop, calls=%fused_computation.clone.1 | loop fusion | flops 4194304 | bytes 4292608 | tf_op jit(solution)/shard_map/while/body/eval_jaxpr/eq | solution.py:72
  116.4 3.1 %select_reduce_fusion.6 = (f32[4,128]{1,0:T(4,128)S(1)}, f32[4,8,128]{2,1,0:T(8,128)S(1)}) fusion(pred[4,128]{1,0:T(4,128)(4,1)S(1)} %broadcast_compare_fusion.4, pred[4,8192,128]{2,1,0:T(32,128)(4,1)S(1)} %bitcast_compare_fusion.2, bf16[16,4,8,8192]{3,2,1,0:T(8,128)(2,1)} %get-tuple-element.118, s32[]{:T(128)} %get-tuple-element.107), kind=kOutput, calls=%fused_computation.7.clone.1 | convolution fusion | flops 67116544 | bytes 4738048 | tf_op jit(solution)/shard_map/while/body/eval_jaxpr/pgk,pkt->pgt/dot_general | solution.py:76
  121.2 2.7 %bitcast_compare_fusion.2 = pred[4,8192,128]{2,1,0:T(32,128)(4,1)S(1)} fusion(s32[8192]{0:T(1024)S(1)} %bitcast.88, s32[4,32,128]{2,1,0:T(8,128)S(1)} %dynamic-slice_bitcast_fusion.6), kind=kLoop, calls=%fused_computation.clone.1 | loop fusion | flops 4194304 | bytes 4292608 | tf_op jit(solution)/shard_map/while/body/eval_jaxpr/eq | solution.py:72
  123.9 3.1 %select_reduce_fusion.6 = (f32[4,128]{1,0:T(4,128)S(1)}, f32[4,8,128]{2,1,0:T(8,128)S(1)}) fusion(pred[4,128]{1,0:T(4,128)(4,1)S(1)} %broadcast_compare_fusion.4, pred[4,8192,128]{2,1,0:T(32,128)(4,1)S(1)} %bitcast_compare_fusion.2, bf16[16,4,8,8192]{3,2,1,0:T(8,128)(2,1)} %get-tuple-element.118, s32[]{:T(128)} %get-tuple-element.107), kind=kOutput, calls=%fused_computation.7.clone.1 | convolution fusion | flops 67116544 | bytes 4738048 | tf_op jit(solution)/shard_map/while/body/eval_jaxpr/pgk,pkt->pgt/dot_general | solution.py:76
  128.7 2.7 %bitcast_compare_fusion.2 = pred[4,8192,128]{2,1,0:T(32,128)(4,1)S(1)} fusion(s32[8192]{0:T(1024)S(1)} %bitcast.88, s32[4,32,128]{2,1,0:T(8,128)S(1)} %dynamic-slice_bitcast_fusion.6), kind=kLoop, calls=%fused_computation.clone.1 | loop fusion | flops 4194304 | bytes 4292608 | tf_op jit(solution)/shard_map/while/body/eval_jaxpr/eq | solution.py:72
  131.4 3.1 %select_reduce_fusion.6 = (f32[4,128]{1,0:T(4,128)S(1)}, f32[4,8,128]{2,1,0:T(8,128)S(1)}) fusion(pred[4,128]{1,0:T(4,128)(4,1)S(1)} %broadcast_compare_fusion.4, pred[4,8192,128]{2,1,0:T(32,128)(4,1)S(1)} %bitcast_compare_fusion.2, bf16[16,4,8,8192]{3,2,1,0:T(8,128)(2,1)} %get-tuple-element.118, s32[]{:T(128)} %get-tuple-element.107), kind=kOutput, calls=%fused_computation.7.clone.1 | convolution fusion | flops 67116544 | bytes 4738048 | tf_op jit(solution)/shard_map/while/body/eval_jaxpr/pgk,pkt->pgt/dot_general | solution.py:76
  136.3 2.7 %bitcast_compare_fusion.2 = pred[4,8192,128]{2,1,0:T(32,128)(4,1)S(1)} fusion(s32[8192]{0:T(1024)S(1)} %bitcast.88, s32[4,32,128]{2,1,0:T(8,128)S(1)} %dynamic-slice_bitcast_fusion.6), kind=kLoop, calls=%fused_computation.clone.1 | loop fusion | flops 4194304 | bytes 4292608 | tf_op jit(solution)/shard_map/while/body/eval_jaxpr/eq | solution.py:72
  138.9 3.1 %select_reduce_fusion.6 = (f32[4,128]{1,0:T(4,128)S(1)}, f32[4,8,128]{2,1,0:T(8,128)S(1)}) fusion(pred[4,128]{1,0:T(4,128)(4,1)S(1)} %broadcast_compare_fusion.4, pred[4,8192,128]{2,1,0:T(32,128)(4,1)S(1)} %bitcast_compare_fusion.2, bf16[16,4,8,8192]{3,2,1,0:T(8,128)(2,1)} %get-tuple-element.118, s32[]{:T(128)} %get-tuple-element.107), kind=kOutput, calls=%fused_computation.7.clone.1 | convolution fusion | flops 67116544 | bytes 4738048 | tf_op jit(solution)/shard_map/while/body/eval_jaxpr/pgk,pkt->pgt/dot_general | solution.py:76
  143.8 2.7 %bitcast_compare_fusion.2 = pred[4,8192,128]{2,1,0:T(32,128)(4,1)S(1)} fusion(s32[8192]{0:T(1024)S(1)} %bitcast.88, s32[4,32,128]{2,1,0:T(8,128)S(1)} %dynamic-slice_bitcast_fusion.6), kind=kLoop, calls=%fused_computation.clone.1 | loop fusion | flops 4194304 | bytes 4292608 | tf_op jit(solution)/shard_map/while/body/eval_jaxpr/eq | solution.py:72
  146.4 3.1 %select_reduce_fusion.6 = (f32[4,128]{1,0:T(4,128)S(1)}, f32[4,8,128]{2,1,0:T(8,128)S(1)}) fusion(pred[4,128]{1,0:T(4,128)(4,1)S(1)} %broadcast_compare_fusion.4, pred[4,8192,128]{2,1,0:T(32,128)(4,1)S(1)} %bitcast_compare_fusion.2, bf16[16,4,8,8192]{3,2,1,0:T(8,128)(2,1)} %get-tuple-element.118, s32[]{:T(128)} %get-tuple-element.107), kind=kOutput, calls=%fused_computation.7.clone.1 | convolution fusion | flops 67116544 | bytes 4738048 | tf_op jit(solution)/shard_map/while/body/eval_jaxpr/pgk,pkt->pgt/dot_general | solution.py:76
  151.3 2.7 %bitcast_compare_fusion.2 = pred[4,8192,128]{2,1,0:T(32,128)(4,1)S(1)} fusion(s32[8192]{0:T(1024)S(1)} %bitcast.88, s32[4,32,128]{2,1,0:T(8,128)S(1)} %dynamic-slice_bitcast_fusion.6), kind=kLoop, calls=%fused_computation.clone.1 | loop fusion | flops 4194304 | bytes 4292608 | tf_op jit(solution)/shard_map/while/body/eval_jaxpr/eq | solution.py:72
  154.0 3.1 %select_reduce_fusion.6 = (f32[4,128]{1,0:T(4,128)S(1)}, f32[4,8,128]{2,1,0:T(8,128)S(1)}) fusion(pred[4,128]{1,0:T(4,128)(4,1)S(1)} %broadcast_compare_fusion.4, pred[4,8192,128]{2,1,0:T(32,128)(4,1)S(1)} %bitcast_compare_fusion.2, bf16[16,4,8,8192]{3,2,1,0:T(8,128)(2,1)} %get-tuple-element.118, s32[]{:T(128)} %get-tuple-element.107), kind=kOutput, calls=%fused_computation.7.clone.1 | convolution fusion | flops 67116544 | bytes 4738048 | tf_op jit(solution)/shard_map/while/body/eval_jaxpr/pgk,pkt->pgt/dot_general | solution.py:76
  158.8 2.7 %bitcast_compare_fusion.2 = pred[4,8192,128]{2,1,0:T(32,128)(4,1)S(1)} fusion(s32[8192]{0:T(1024)S(1)} %bitcast.88, s32[4,32,128]{2,1,0:T(8,128)S(1)} %dynamic-slice_bitcast_fusion.6), kind=kLoop, calls=%fused_computation.clone.1 | loop fusion | flops 4194304 | bytes 4292608 | tf_op jit(solution)/shard_map/while/body/eval_jaxpr/eq | solution.py:72
  161.5 3.1 %select_reduce_fusion.6 = (f32[4,128]{1,0:T(4,128)S(1)}, f32[4,8,128]{2,1,0:T(8,128)S(1)}) fusion(pred[4,128]{1,0:T(4,128)(4,1)S(1)} %broadcast_compare_fusion.4, pred[4,8192,128]{2,1,0:T(32,128)(4,1)S(1)} %bitcast_compare_fusion.2, bf16[16,4,8,8192]{3,2,1,0:T(8,128)(2,1)} %get-tuple-element.118, s32[]{:T(128)} %get-tuple-element.107), kind=kOutput, calls=%fused_computation.7.clone.1 | convolution fusion | flops 67116544 | bytes 4738048 | tf_op jit(solution)/shard_map/while/body/eval_jaxpr/pgk,pkt->pgt/dot_general | solution.py:76
  166.3 2.7 %bitcast_compare_fusion.2 = pred[4,8192,128]{2,1,0:T(32,128)(4,1)S(1)} fusion(s32[8192]{0:T(1024)S(1)} %bitcast.88, s32[4,32,128]{2,1,0:T(8,128)S(1)} %dynamic-slice_bitcast_fusion.6), kind=kLoop, calls=%fused_computation.clone.1 | loop fusion | flops 4194304 | bytes 4292608 | tf_op jit(solution)/shard_map/while/body/eval_jaxpr/eq | solution.py:72
  169.0 3.1 %select_reduce_fusion.6 = (f32[4,128]{1,0:T(4,128)S(1)}, f32[4,8,128]{2,1,0:T(8,128)S(1)}) fusion(pred[4,128]{1,0:T(4,128)(4,1)S(1)} %broadcast_compare_fusion.4, pred[4,8192,128]{2,1,0:T(32,128)(4,1)S(1)} %bitcast_compare_fusion.2, bf16[16,4,8,8192]{3,2,1,0:T(8,128)(2,1)} %get-tuple-element.118, s32[]{:T(128)} %get-tuple-element.107), kind=kOutput, calls=%fused_computation.7.clone.1 | convolution fusion | flops 67116544 | bytes 4738048 | tf_op jit(solution)/shard_map/while/body/eval_jaxpr/pgk,pkt->pgt/dot_general | solution.py:76
  173.8 2.7 %bitcast_compare_fusion.2 = pred[4,8192,128]{2,1,0:T(32,128)(4,1)S(1)} fusion(s32[8192]{0:T(1024)S(1)} %bitcast.88, s32[4,32,128]{2,1,0:T(8,128)S(1)} %dynamic-slice_bitcast_fusion.6), kind=kLoop, calls=%fused_computation.clone.1 | loop fusion | flops 4194304 | bytes 4292608 | tf_op jit(solution)/shard_map/while/body/eval_jaxpr/eq | solution.py:72
  176.5 3.1 %select_reduce_fusion.6 = (f32[4,128]{1,0:T(4,128)S(1)}, f32[4,8,128]{2,1,0:T(8,128)S(1)}) fusion(pred[4,128]{1,0:T(4,128)(4,1)S(1)} %broadcast_compare_fusion.4, pred[4,8192,128]{2,1,0:T(32,128)(4,1)S(1)} %bitcast_compare_fusion.2, bf16[16,4,8,8192]{3,2,1,0:T(8,128)(2,1)} %get-tuple-element.118, s32[]{:T(128)} %get-tuple-element.107), kind=kOutput, calls=%fused_computation.7.clone.1 | convolution fusion | flops 67116544 | bytes 4738048 | tf_op jit(solution)/shard_map/while/body/eval_jaxpr/pgk,pkt->pgt/dot_general | solution.py:76
  181.4 2.7 %bitcast_compare_fusion.2 = pred[4,8192,128]{2,1,0:T(32,128)(4,1)S(1)} fusion(s32[8192]{0:T(1024)S(1)} %bitcast.88, s32[4,32,128]{2,1,0:T(8,128)S(1)} %dynamic-slice_bitcast_fusion.6), kind=kLoop, calls=%fused_computation.clone.1 | loop fusion | flops 4194304 | bytes 4292608 | tf_op jit(solution)/shard_map/while/body/eval_jaxpr/eq | solution.py:72
  184.0 3.1 %select_reduce_fusion.6 = (f32[4,128]{1,0:T(4,128)S(1)}, f32[4,8,128]{2,1,0:T(8,128)S(1)}) fusion(pred[4,128]{1,0:T(4,128)(4,1)S(1)} %broadcast_compare_fusion.4, pred[4,8192,128]{2,1,0:T(32,128)(4,1)S(1)} %bitcast_compare_fusion.2, bf16[16,4,8,8192]{3,2,1,0:T(8,128)(2,1)} %get-tuple-element.118, s32[]{:T(128)} %get-tuple-element.107), kind=kOutput, calls=%fused_computation.7.clone.1 | convolution fusion | flops 67116544 | bytes 4738048 | tf_op jit(solution)/shard_map/while/body/eval_jaxpr/pgk,pkt->pgt/dot_general | solution.py:76
  188.9 2.7 %bitcast_compare_fusion.2 = pred[4,8192,128]{2,1,0:T(32,128)(4,1)S(1)} fusion(s32[8192]{0:T(1024)S(1)} %bitcast.88, s32[4,32,128]{2,1,0:T(8,128)S(1)} %dynamic-slice_bitcast_fusion.6), kind=kLoop, calls=%fused_computation.clone.1 | loop fusion | flops 4194304 | bytes 4292608 | tf_op jit(solution)/shard_map/while/body/eval_jaxpr/eq | solution.py:72
  191.6 3.1 %select_reduce_fusion.6 = (f32[4,128]{1,0:T(4,128)S(1)}, f32[4,8,128]{2,1,0:T(8,128)S(1)}) fusion(pred[4,128]{1,0:T(4,128)(4,1)S(1)} %broadcast_compare_fusion.4, pred[4,8192,128]{2,1,0:T(32,128)(4,1)S(1)} %bitcast_compare_fusion.2, bf16[16,4,8,8192]{3,2,1,0:T(8,128)(2,1)} %get-tuple-element.118, s32[]{:T(128)} %get-tuple-element.107), kind=kOutput, calls=%fused_computation.7.clone.1 | convolution fusion | flops 67116544 | bytes 4738048 | tf_op jit(solution)/shard_map/while/body/eval_jaxpr/pgk,pkt->pgt/dot_general | solution.py:76
  196.4 2.7 %bitcast_compare_fusion.2 = pred[4,8192,128]{2,1,0:T(32,128)(4,1)S(1)} fusion(s32[8192]{0:T(1024)S(1)} %bitcast.88, s32[4,32,128]{2,1,0:T(8,128)S(1)} %dynamic-slice_bitcast_fusion.6), kind=kLoop, calls=%fused_computation.clone.1 | loop fusion | flops 4194304 | bytes 4292608 | tf_op jit(solution)/shard_map/while/body/eval_jaxpr/eq | solution.py:72
  199.1 3.1 %select_reduce_fusion.6 = (f32[4,128]{1,0:T(4,128)S(1)}, f32[4,8,128]{2,1,0:T(8,128)S(1)}) fusion(pred[4,128]{1,0:T(4,128)(4,1)S(1)} %broadcast_compare_fusion.4, pred[4,8192,128]{2,1,0:T(32,128)(4,1)S(1)} %bitcast_compare_fusion.2, bf16[16,4,8,8192]{3,2,1,0:T(8,128)(2,1)} %get-tuple-element.118, s32[]{:T(128)} %get-tuple-element.107), kind=kOutput, calls=%fused_computation.7.clone.1 | convolution fusion | flops 67116544 | bytes 4738048 | tf_op jit(solution)/shard_map/while/body/eval_jaxpr/pgk,pkt->pgt/dot_general | solution.py:76
  203.9 2.8 %copy.64 = bf16[4,64,2048]{2,1,0:T(8,128)(2,1)} copy(bf16[4,64,2048]{2,0,1:T(4,128)(2,1)} %all-to-all-done.1) | data formatting | bytes 2097152 | tf_op jit(solution)/shard_map/all_to_all | solution.py:104
  215.5 10.3 %all-to-all-start.3 = ((bf16[64,2,512]{2,1,0:T(2,128)(2,1)}), bf16[64,2,512]{2,1,0:T(2,128)(2,1)S(1)}, u32[]{:S(2)}, u32[]{:S(2)}) async-start(bf16[64,2,512]{2,1,0:T(2,128)(2,1)} %reshape.228), calls=%async_computation.3 | async-start | bytes 262144 | tf_op jit(solution)/shard_map/all_to_all | solution.py:116
  228.4 7.3 %all-to-all-done.3 = bf16[64,2,512]{2,1,0:T(2,128)(2,1)S(1)} async-done(((bf16[64,2,512]{2,1,0:T(2,128)(2,1)}), bf16[64,2,512]{2,1,0:T(2,128)(2,1)S(1)}, u32[]{:S(2)}, u32[]{:S(2)}) %all-to-all-start.3) | async-done | bytes 131104 | tf_op jit(solution)/shard_map/all_to_all | solution.py:116
  236.1 16.9 %all-reduce = bf16[32,128]{1,0:T(8,128)(2,1)S(1)} all-reduce(f32[32,128]{1,0:T(8,128)S(1)} %reduce_sum.75), channel_id=2, replica_groups=mesh['seq'=64,'head'=4] {'head'}, use_global_device_ids=true, to_apply=%region_15.16.clone | all-reduce | flops 4096 | bytes 24576
  (331 shorter events, 45.1 us)
Async XLA Ops:
  0.6 235.2 %copy-start = (bf16[2048,128]{1,0:T(8,128)(2,1)S(1)}, bf16[2048,128]{1,0:T(8,128)(2,1)}, u32[]{:S(2)}) copy-start(bf16[2048,128]{1,0:T(8,128)(2,1)} %param.17) | copy-start | bytes 1572868
  4.7 20.7 %all-to-all-start = ((bf16[4,64,1]{0,2,1:T(2,128)(2,1)}), bf16[4,64,1]{0,2,1:T(2,128)(2,1)S(1)}, u32[]{:S(2)}, u32[]{:S(2)}) async-start(bf16[4,64,1]{0,2,1:T(2,128)(2,1)} %copy.62), calls=%async_computation | async-start | bytes 65536 | tf_op jit(solution)/shard_map/all_to_all | solution.py:106
  16.8 15.2 %copy-start.2 = (s32[32,8]{0,1:T(8,128)S(1)}, s32[32,8]{0,1:T(8,128)}, u32[]{:S(2)}) copy-start(s32[32,8]{0,1:T(8,128)} %param.16) | copy-start | bytes 3076
  21.4 15.0 %copy-start.1 = (f32[2,4,32,256]{3,2,1,0:T(8,128)S(1)}, f32[2,4,32,256]{3,2,1,0:T(8,128)}, u32[]{:S(2)}) copy-start(f32[2,4,32,256]{3,2,1,0:T(8,128)} %param.14) | copy-start | bytes 786436
  25.5 46.7 %all-to-all-start.1 = ((bf16[4,64,2048]{2,0,1:T(4,128)(2,1)}), bf16[4,64,2048]{2,0,1:T(4,128)(2,1)}, u32[]{:S(2)}, u32[]{:S(2)}) async-start(bf16[4,64,2048]{2,0,1:T(4,128)(2,1)} %fusion.5), calls=%async_computation.1 | async-start | bytes 2097152 | tf_op jit(solution)/shard_map/all_to_all | solution.py:104
  72.1 136.1 %all-to-all-start.2 = ((bf16[4,64,2048]{2,0,1:T(4,128)(2,1)}), bf16[4,64,2048]{2,0,1:T(4,128)(2,1)S(1)}, u32[]{:S(2)}, u32[]{:S(2)}) async-start(bf16[4,64,2048]{2,0,1:T(4,128)(2,1)} %fusion.6), calls=%async_computation.2 | async-start | bytes 2097152 | tf_op jit(solution)/shard_map/all_to_all | solution.py:105
  208.3 18.3 %copy-start.3 = (u32[256]{0:T(256)S(1)}, u32[256]{0:T(256)}, u32[]{:S(2)}) copy-start(u32[256]{0:T(256)} %constant.73) | copy-start | bytes 3076
  215.5 20.2 %all-to-all-start.3 = ((bf16[64,2,512]{2,1,0:T(2,128)(2,1)}), bf16[64,2,512]{2,1,0:T(2,128)(2,1)S(1)}, u32[]{:S(2)}, u32[]{:S(2)}) async-start(bf16[64,2,512]{2,1,0:T(2,128)(2,1)} %reshape.228), calls=%async_computation.3 | async-start | bytes 262144 | tf_op jit(solution)/shard_map/all_to_all | solution.py:116
